TPU v7x, 512 devices: a whole 4x8x8 slice. The times are simulated.
512 devices in a mesh: pp: 16 (over z, core), ep: 32 (over x, y).
Axes of the slice: x: 4, y: 8, z: 8, core: 2. Of those that a mesh axis runs over, the one named last changes fastest.
Arguments:
- pending_activations: bfloat16 [16, 2048, 3584], P('pp', 'ep'), may hold values from -6 to 6
- incoming_microbatches: bfloat16 [1, 2048, 3584], P(None, 'ep'), may hold values from -6 to 6
- layer_rescale_factor: float32 [16, 3584], P('pp'), may hold values from 0.5 to 1.5
- gating_projection_matrix: bfloat16 [16, 3584, 4096], P('pp', None, 'ep'), may hold values from -0.09375 to 0.09375
- widening_projection_matrix: bfloat16 [16, 3584, 4096], P('pp', None, 'ep'), may hold values from -0.09375 to 0.09375
- output_projection_matrix: bfloat16 [16, 4096, 3584], P('pp', 'ep'), may hold values from -0.1875 to 0.1875
- picked_specialist_ids: int32 [2, 16, 2048, 1], P(None, 'pp', 'ep'), may hold values from 0 to 3; in each aligned block of 64 rows (0 to 63, 64 to 127, ..., all dimensions but the last counted through in order) at most 17 rows name the same one
- dispatcher_probability_values: float32 [2, 16, 2048, 1], P(None, 'pp', 'ep'), may hold values from 0.1 to 1
Outputs:
- section_outputs: bfloat16 [2, 16, 2048, 3584], P(None, 'pp', 'ep')
Inputs may be any that keep to these rules, and one draw needn't show every extreme that they name: `picked_specialist_ids`: each token names exactly one expert. In each step and section, the 64 rows of one device (aligned blocks of the token dimension) name each expert at most 17 times, a bound that some block reaches.
All inputs are finite; a program needn't handle non-finite values.
Results may differ from a plain program's by a relative error of at most 0.0055.
Values may be sent and summed in bfloat16 or wider, within the bound.
No kernel may reach another device: no remote copies, remote signals or barrier semaphores. Data moves between devices by JAX's collectives and lax.ppermute only.
A program may use at most 64 MiB of HBM per device.

v0:
```python
import jax
import jax.numpy as jnp
from jax import lax
from jax.sharding import Mesh, PartitionSpec as P

GROUP = 8


def slots_of(chosen, slot_count, experts):
    hits = (chosen[:, None] == jnp.arange(experts, dtype=jnp.int32)[None, :]).astype(jnp.int32)
    before = jnp.cumsum(hits, axis=0) - hits
    return chosen * slot_count + jnp.sum(before * hits, axis=1)


def section_layer(inputs, gain_row, gate_w, up_w, down_w, chosen, scores):
    row_count, width = inputs.shape
    experts = lax.axis_size("x")
    ring = lax.axis_size("y")
    slot_count = 17
    float_rows = inputs.astype(jnp.float32)
    variance = jnp.mean(float_rows * float_rows, axis=-1, keepdims=True)
    normed = (float_rows * lax.rsqrt(variance + 1e-06) * gain_row).astype(jnp.bfloat16)
    slot_ids = slots_of(chosen[:, 0], slot_count, experts)
    slot_grid = jnp.arange(experts * slot_count, dtype=jnp.int32)
    picker = (slot_grid[:, None] == slot_ids[None, :]).astype(jnp.bfloat16)
    packed = jnp.dot(picker, normed, preferred_element_type=jnp.float32).astype(jnp.bfloat16)
    sent = packed.reshape(experts, slot_count, width)
    mine = lax.all_to_all(sent, "x", split_axis=0, concat_axis=0, tiled=True)
    mine = mine.reshape(experts * slot_count, width)
    held = experts * slot_count
    padded = -(-held // 8) * 8
    mine = jnp.pad(mine, ((0, padded - held), (0, 0)))
    rows = lax.all_gather(mine, "y", axis=0, tiled=True)
    gate_val = jnp.dot(rows, gate_w, preferred_element_type=jnp.float32)
    up_val = jnp.dot(rows, up_w, preferred_element_type=jnp.float32)
    active = (jax.nn.silu(gate_val) * up_val).astype(jnp.bfloat16)
    partial = jnp.dot(active, down_w, preferred_element_type=jnp.float32).astype(jnp.bfloat16)
    summed = lax.psum_scatter(partial, "y", scatter_dimension=0, tiled=True)
    back = summed[:held].reshape(experts, slot_count, width)
    back = lax.all_to_all(back, "x", split_axis=0, concat_axis=0, tiled=True)
    back = back.reshape(held, width)
    unpick = (slot_ids[:, None] == slot_grid[None, :]).astype(jnp.bfloat16)
    combined = scores * jnp.dot(unpick, back, preferred_element_type=jnp.float32)
    return (float_rows + combined).astype(jnp.bfloat16)


def local(pending, incoming, gain, gate_w, up_w, down_w, chosen, scores):
    tick_total = chosen.shape[0]
    first_section = lax.axis_index("pp") == 0
    count = lax.axis_size("pp")
    rows = pending[0]
    outputs = []
    for tick in range(tick_total):
        produced = section_layer(
            rows, gain[0], gate_w[0], up_w[0], down_w[0], chosen[tick, 0], scores[tick, 0]
        )
        outputs.append(produced)
        if tick + 1 < tick_total:
            passed = lax.ppermute(produced, "pp", [(i, i + 1) for i in range(count - 1)])
            rows = jnp.where(first_section, incoming[tick], passed)
    return jnp.stack(outputs)[:, None]


def solution(mesh):
    fine = Mesh(mesh.devices.reshape(mesh.shape["pp"], -1, GROUP), ("pp", "x", "y"))
    ep = ("x", "y")
    in_specs = (
        P("pp", ep, None),
        P(None, ep, None),
        P("pp", None),
        P("pp", None, ep),
        P("pp", None, ep),
        P("pp", ep, None),
        P(None, "pp", ep, None),
        P(None, "pp", ep, None),
    )
    out_specs = P(None, "pp", ep, None)
    return jax.shard_map(local, mesh=fine, in_specs=in_specs, out_specs=out_specs, check_vma=False)
```

profile of v0, /device:TPU:24, one launch (start us, length us, event | category | flops | bytes accessed | tf_op | source)
XLA Modules:
  0.0 347.5 jit_solution(16498930131038805519)
XLA Ops:
  6.5 1.3 fusion.10
  7.8 0.7 slice_bitcast_fusion
  8.9 0.8 reduce
  9.6 0.2 select_reduce_fusion
  9.8 0.7 multiply_add_fusion
  10.5 1.4 convolution_convert_fusion.3
  12.0 15.3 %all_to_all.20 = bf16[4,17,3584]{2,1,0:T(8,128)(2,1)S(1)} all-to-all(bf16[4,17,3584]{2,1,0:T(8,128)(2,1)S(1)} %reshape.78), channel_id=1, replica_groups=mesh['pp'=16,'x'=4,'y'=8] {'x'}, dimensions={0} | all-to-all | bytes 974848 | tf_op jit(solution)/shard_map/all_to_all | solution.py:28
  27.5 0.8 pad.7
  28.4 58.9 %all-gather.3.cloned.1.call-done = bf16[576,3584]{1,0:T(8,128)(2,1)} async-done(((bf16[72,3584]{1,0:T(8,128)(2,1)}), bf16[576,3584]{1,0:T(8,128)(2,1)}) %all-gather.3.cloned.1.call-update) | async-done | bytes 4128784 | tf_op jit(solution)/shard_map/all_gather | solution.py:33
  87.4 3.6 %fusion.21 = f32[576,128]{1,0:T(8,128)S(1)} fusion(bf16[576,3584]{1,0:T(8,128)(2,1)} %all-gather.3.cloned.1.call-done, bf16[1,3584,128]{2,1,0:T(8,128)(2,1)} %param.11), kind=kOutput, calls=%fused_computation.32 | convolution fusion | flops 528482304 | bytes 5341184 | tf_op jit(solution)/shard_map/dot_general | solution.py:34
  91.0 8.5 %convolution_convert_fusion.1 = bf16[576,3584]{1,0:T(8,128)(2,1)} fusion(bf16[576,3584]{1,0:T(8,128)(2,1)} %all-gather.3.cloned.1.call-done, bf16[1,128,3584]{2,1,0:T(8,128)(2,1)S(1)} %copy-done, bf16[1,3584,128]{2,1,0:T(8,128)(2,1)S(1)} %copy-done.2, f32[576,128]{1,0:T(8,128)S(1)} %fusion.21), kind=kOutput, calls=%fused_computation.1 | convolution fusion | flops 1059471360 | bytes 10387456 | tf_op jit(solution)/shard_map/dot_general | solution.py:37
  99.5 56.3 %reduce-scatter.3.cloned.1.call-done = bf16[72,3584]{1,0:T(8,128)(2,1)} async-done(((bf16[576,3584]{1,0:T(8,128)(2,1)}), bf16[72,3584]{1,0:T(8,128)(2,1)}) %reduce-scatter.3.cloned.1.call-update) | async-done | bytes 516112 | tf_op jit(solution)/shard_map/reduce_scatter | solution.py:38
  155.8 2.0 reshape.80
  157.9 4.2 %all-to-all-start.1 = ((bf16[4,17,3584]{2,1,0:T(8,128)(2,1)}), bf16[4,17,3584]{2,1,0:T(8,128)(2,1)S(1)}, u32[]{:S(2)}, u32[]{:S(2)}) async-start(bf16[4,17,3584]{2,1,0:T(8,128)(2,1)} %reshape.80), calls=%async_computation.2 | async-start | bytes 1376256 | tf_op jit(solution)/shard_map/all_to_all | solution.py:40
  162.1 11.1 %all-to-all-done.1 = bf16[4,17,3584]{2,1,0:T(8,128)(2,1)S(1)} async-done(((bf16[4,17,3584]{2,1,0:T(8,128)(2,1)}), bf16[4,17,3584]{2,1,0:T(8,128)(2,1)S(1)}, u32[]{:S(2)}, u32[]{:S(2)}) %all-to-all-start.1) | async-done | bytes 487456 | tf_op jit(solution)/shard_map/all_to_all | solution.py:40
  173.4 0.3 fusion.3
  173.8 1.3 collective-permute-start
  175.1 1.4 collective-permute-done
  176.5 1.3 fusion.7
  177.8 0.4 convolution_convert_fusion.2
  178.2 0.2 reshape.82
  178.3 12.1 %all_to_all.21 = bf16[4,17,3584]{2,1,0:T(8,128)(2,1)} all-to-all(bf16[4,17,3584]{2,1,0:T(8,128)(2,1)S(1)} %reshape.82), channel_id=1, replica_groups=mesh['pp'=16,'x'=4,'y'=8] {'x'}, dimensions={0} | all-to-all | bytes 974848 | tf_op jit(solution)/shard_map/all_to_all | solution.py:28
  190.4 1.3 reshape.83
  191.7 0.8 pad.8
  192.6 62.1 %all-gather.5.cloned.1.call-done = bf16[576,3584]{1,0:T(8,128)(2,1)} async-done(((bf16[72,3584]{1,0:T(8,128)(2,1)}), bf16[576,3584]{1,0:T(8,128)(2,1)}) %all-gather.5.cloned.1.call-update) | async-done | bytes 4128784 | tf_op jit(solution)/shard_map/all_gather | solution.py:33
  254.6 3.6 %fusion.19 = f32[576,128]{1,0:T(8,128)S(1)} fusion(bf16[576,3584]{1,0:T(8,128)(2,1)} %all-gather.5.cloned.1.call-done, bf16[1,3584,128]{2,1,0:T(8,128)(2,1)} %param.11), kind=kOutput, calls=%fused_computation.30 | convolution fusion | flops 528482304 | bytes 5341184 | tf_op jit(solution)/shard_map/dot_general | solution.py:34
  258.3 8.5 %convolution_convert_fusion = bf16[576,3584]{1,0:T(8,128)(2,1)} fusion(bf16[576,3584]{1,0:T(8,128)(2,1)} %all-gather.5.cloned.1.call-done, bf16[1,128,3584]{2,1,0:T(8,128)(2,1)S(1)} %copy-done, bf16[1,3584,128]{2,1,0:T(8,128)(2,1)S(1)} %copy-done.2, f32[576,128]{1,0:T(8,128)S(1)} %fusion.19), kind=kOutput, calls=%fused_computation | convolution fusion | flops 1059471360 | bytes 10387456 | tf_op jit(solution)/shard_map/dot_general | solution.py:37
  266.8 56.3 %reduce-scatter.5.cloned.1.call-done = bf16[72,3584]{1,0:T(8,128)(2,1)} async-done(((bf16[576,3584]{1,0:T(8,128)(2,1)}), bf16[72,3584]{1,0:T(8,128)(2,1)}) %reduce-scatter.5.cloned.1.call-update) | async-done | bytes 516112 | tf_op jit(solution)/shard_map/reduce_scatter | solution.py:38
  323.1 1.2 reshape.84
  324.3 15.2 %all_to_all.22 = bf16[4,17,3584]{2,1,0:T(8,128)(2,1)S(1)} all-to-all(bf16[4,17,3584]{2,1,0:T(8,128)(2,1)S(1)} %reshape.84), channel_id=1, replica_groups=mesh['pp'=16,'x'=4,'y'=8] {'x'}, dimensions={0} | all-to-all | bytes 974848 | tf_op jit(solution)/shard_map/all_to_all | solution.py:40
  339.6 0.3 fusion.4
  340.0 1.0 maximum_bitcast_fusion
  (31 shorter events, 1.2 us)
Async XLA Ops:
  6.5 84.5 %copy-start = (bf16[1,128,3584]{2,1,0:T(8,128)(2,1)S(1)}, bf16[1,128,3584]{2,1,0:T(8,128)(2,1)}, u32[]{:S(2)}) copy-start(bf16[1,128,3584]{2,1,0:T(8,128)(2,1)} %param.13) | copy-start | bytes 2752516
  6.5 80.8 %all-gather.3.cloned.1.call-start = ((), (), s32[]{:S(2)}) async-start(), calls=%async_computation.6 | async-start | bytes 4644864 | tf_op jit(solution)/shard_map/all_gather | solution.py:33
  27.5 63.5 %copy-start.2 = (bf16[1,3584,128]{2,1,0:T(8,128)(2,1)S(1)}, bf16[1,3584,128]{2,1,0:T(8,128)(2,1)}, u32[]{:S(2)}) copy-start(bf16[1,3584,128]{2,1,0:T(8,128)(2,1)} %param.12) | copy-start | bytes 2752516
  28.4 127.4 %reduce-scatter.3.cloned.1.call-start = ((), (), s32[]{:S(2)}) async-start(), calls=%async_computation.7 | async-start | bytes 4644864 | tf_op jit(solution)/shard_map/reduce_scatter | solution.py:38
  99.5 62.6 %copy-start.5 = (f32[2,1,64,1]{2,3,1,0:T(1,128)S(1)}, f32[2,1,64,1]{2,3,1,0:T(1,128)}, u32[]{:S(2)}) copy-start(f32[2,1,64,1]{2,3,1,0:T(1,128)} %param.15) | copy-start | bytes 1540
  99.5 73.9 %copy-start.1 = (bf16[1,64,3584]{2,1,0:T(8,128)(2,1)S(1)}, bf16[1,64,3584]{2,1,0:T(8,128)(2,1)}, u32[]{:S(2)}) copy-start(bf16[1,64,3584]{2,1,0:T(8,128)(2,1)} %param.8) | copy-start | bytes 1376260
  157.9 15.4 %all-to-all-start.1 = ((bf16[4,17,3584]{2,1,0:T(8,128)(2,1)}), bf16[4,17,3584]{2,1,0:T(8,128)(2,1)S(1)}, u32[]{:S(2)}, u32[]{:S(2)}) async-start(bf16[4,17,3584]{2,1,0:T(8,128)(2,1)} %reshape.80), calls=%async_computation.2 | async-start | bytes 1376256 | tf_op jit(solution)/shard_map/all_to_all | solution.py:40
  162.1 92.5 %all-gather.5.cloned.1.call-start = ((), (), s32[]{:S(2)}) async-start(), calls=%async_computation.8 | async-start | bytes 4644864 | tf_op jit(solution)/shard_map/all_gather | solution.py:33
  173.8 4.0 %copy-start.3 = (bf16[64,3584]{1,0:T(8,128)(2,1)}, bf16[64,3584]{1,0:T(8,128)(2,1)S(1)}, u32[]{:S(2)}) copy-start(bf16[64,3584]{1,0:T(8,128)(2,1)S(1)} %fusion.3) | copy-start | bytes 1376260
  173.8 2.7 collective-permute-start
  192.5 130.5 %reduce-scatter.5.cloned.1.call-start = ((), (), s32[]{:S(2)}) async-start(), calls=%async_computation.9 | async-start | bytes 4644864 | tf_op jit(solution)/shard_map/reduce_scatter | solution.py:38
  266.8 73.2 %copy-start.4 = (bf16[64,3584]{1,0:T(8,128)(2,1)S(1)}, bf16[64,3584]{1,0:T(8,128)(2,1)}, u32[]{:S(2)}) copy-start(bf16[64,3584]{1,0:T(8,128)(2,1)} %copy-done.3) | copy-start | bytes 1376260
Sparse Core Ops, SparseCore 0:
  28.5 58.7 all-gather.2
  99.7 56.0 reduce-scatter.2
  192.6 61.9 all-gather.4
  266.9 56.0 reduce-scatter.4
where the time goes:
time: 348 us
  waiting for transfers between devices  246 us (71%)
  blocking collectives  42.6 us (12%)
  matrix products  26.7 us (8%)
  between operations  13.3 us (4%)
  local copies, waits for them, and re-layouts  7.68 us (2%)
  starting transfers between devices  5.65 us (2%)
  other arithmetic  5.54 us (2%)
    all_gather x2, waiting for transfers between devices, section_layer(): rows = lax.all_gather(mine, 'y', axis=0, tiled=True)  121 us
    reduce_scatter x2, waiting for transfers between devices, section_layer(): summed = lax.psum_scatter(partial, 'y', scatter_dimension=0, tiled=True)  113 us
    all_to_all x2, blocking collectives, section_layer(): mine = lax.all_to_all(sent, 'x', split_axis=0, concat_axis=0, tiled=True)  27.4 us
    dot_general x2, matrix products, section_layer(): jnp.dot(active, down_w, preferred_element_type=jnp.float32)  17 us
    all_to_all x1, blocking collectives, section_layer(): back = lax.all_to_all(back, 'x', split_axis=0, concat_axis=0, tiled=True)  15.2 us
    all_to_all x1, waiting for transfers between devices, section_layer(): back = lax.all_to_all(back, 'x', split_axis=0, concat_axis=0, tiled=True)  11.1 us
    dot_general x2, matrix products, section_layer(): gate_val = jnp.dot(rows, gate_w, preferred_element_type=jnp.float32)  7.29 us
  transfers between devices with their start and end apart: 6, of which 6 were waited for; matrix products, arithmetic and copies ran while one was open for 0% of the time, Pallas kernels for 0%

commit v1 on v0

--- a/solution.py
+++ b/solution.py
@@ -30,7 +30,9 @@
     held = experts * slot_count
     padded = -(-held // 8) * 8
     mine = jnp.pad(mine, ((0, padded - held), (0, 0)))
-    rows = lax.all_gather(mine, "y", axis=0, tiled=True)
+    rows = jnp.concatenate(
+        lax.all_to_all(jnp.stack([mine] * lax.axis_size("y")), "y", 0, 0), axis=0
+    )
     gate_val = jnp.dot(rows, gate_w, preferred_element_type=jnp.float32)
     up_val = jnp.dot(rows, up_w, preferred_element_type=jnp.float32)
     active = (jax.nn.silu(gate_val) * up_val).astype(jnp.bfloat16)

time: 348 us -> 427 us (1.23)
  blocking collectives: 42.6 us -> 234 us
  waiting for transfers between devices: 246 us -> 134 us
  matrix products: 26.7 us -> 21.8 us
    all_to_all x0 -> x2, blocking collectives: none -> 192 us  [section_layer(): lax.all_to_all(jnp.stack([mine] * lax.axis_size('y')), 'y', 0, 0)]
    all_gather x2 -> x0, waiting for transfers between devices: 121 us -> none  [section_layer(): rows = lax.all_gather(mine, 'y', axis=0, tiled=True)]
    reduce_scatter x2, waiting for transfers between devices: 113 us -> 122 us  [section_layer(): summed = lax.psum_scatter(partial, 'y', scatter_dimension=0, tiled=True)]
    dot_general x2, matrix products: 7.29 us -> 2.47 us  [section_layer(): gate_val = jnp.dot(rows, gate_w, preferred_element_type=jnp.float32)]
  transfers between devices with their start and end apart: 6 -> 4, of which waited for: 6 -> 4; matrix products, arithmetic and copies ran while one was open for 0% -> 0% of each run, Pallas kernels for 0% -> 0%
where the time goes in v1:
time: 427 us; the launch traced here: 426 us
  blocking collectives  234 us (55%)
  waiting for transfers between devices  134 us (31%)
  matrix products  21.8 us (5%)
  between operations  13.6 us (3%)
  local copies, waits for them, and re-layouts  10.5 us (2%)
  starting transfers between devices  5.56 us (1%)
  other arithmetic  5.54 us (1%)
    all_to_all x2, blocking collectives, section_layer(): lax.all_to_all(jnp.stack([mine] * lax.axis_size('y')), 'y', 0, 0)  192 us
    reduce_scatter x2, waiting for transfers between devices, section_layer(): summed = lax.psum_scatter(partial, 'y', scatter_dimension=0, tiled=True)  122 us
    all_to_all x2, blocking collectives, section_layer(): mine = lax.all_to_all(sent, 'x', split_axis=0, concat_axis=0, tiled=True)  27.4 us
    dot_general x2, matrix products, section_layer(): jnp.dot(active, down_w, preferred_element_type=jnp.float32)  17 us
    all_to_all x1, blocking collectives, section_layer(): back = lax.all_to_all(back, 'x', split_axis=0, concat_axis=0, tiled=True)  15.2 us
    all_to_all x1, waiting for transfers between devices, section_layer(): back = lax.all_to_all(back, 'x', split_axis=0, concat_axis=0, tiled=True)  11.2 us
  transfers between devices with their start and end apart: 4, of which 4 were waited for; matrix products, arithmetic and copies ran while one was open for 0% of the time, Pallas kernels for 0%

profile of v1, /device:TPU:24, one launch (start us, length us, event | category | flops | bytes accessed | tf_op | source)
XLA Modules:
  0.0 425.7 jit_solution(9548368392726385940)
XLA Ops:
  6.5 1.3 fusion.10
  7.8 0.7 slice_bitcast_fusion
  8.9 0.8 reduce
  9.8 0.7 multiply_add_fusion
  10.5 1.4 convolution_convert_fusion.3
  12.0 15.3 %all_to_all.30 = bf16[4,17,3584]{2,1,0:T(8,128)(2,1)S(1)} all-to-all(bf16[4,17,3584]{2,1,0:T(8,128)(2,1)S(1)} %reshape.88), channel_id=1, replica_groups=mesh['pp'=16,'x'=4,'y'=8] {'x'}, dimensions={0} | all-to-all | bytes 974848 | tf_op jit(solution)/shard_map/all_to_all | solution.py:28
  27.6 0.3 stack.10
  27.9 97.1 %all_to_all.31 = bf16[8,72,3584]{2,1,0:T(8,128)(2,1)S(1)} all-to-all(bf16[8,72,3584]{2,1,0:T(8,128)(2,1)S(1)} %stack.10), channel_id=1, replica_groups=mesh['pp'=16,'x'=4,'y'=8] {'y'}, dimensions={0} | all-to-all | bytes 8257536 | tf_op jit(solution)/shard_map/all_to_all | solution.py:34
  125.0 1.9 copy-done.1
  126.9 1.2 fusion.21
  128.2 8.5 %convolution_convert_fusion.1 = bf16[576,3584]{1,0:T(8,128)(2,1)} fusion(bf16[576,3584]{1,0:T(8,128)(2,1)} %bitcast.58, bf16[1,128,3584]{2,1,0:T(8,128)(2,1)S(1)} %copy-done, bf16[1,3584,128]{2,1,0:T(8,128)(2,1)S(1)} %copy-done.4, f32[576,128]{1,0:T(8,128)S(1)} %fusion.21), kind=kOutput, calls=%fused_computation.1 | convolution fusion | flops 1059471360 | bytes 10387456 | tf_op jit(solution)/shard_map/dot_general | solution.py:39
  136.7 57.6 %reduce-scatter.3.cloned.1.call-done = bf16[72,3584]{1,0:T(8,128)(2,1)} async-done(((bf16[576,3584]{1,0:T(8,128)(2,1)}), bf16[72,3584]{1,0:T(8,128)(2,1)}) %reduce-scatter.3.cloned.1.call-update) | async-done | bytes 516112 | tf_op jit(solution)/shard_map/reduce_scatter | solution.py:40
  194.3 2.0 reshape.91
  196.4 4.2 all-to-all-start.2
  200.6 11.2 %all-to-all-done.2 = bf16[4,17,3584]{2,1,0:T(8,128)(2,1)S(1)} async-done(((bf16[4,17,3584]{2,1,0:T(8,128)(2,1)}), bf16[4,17,3584]{2,1,0:T(8,128)(2,1)S(1)}, u32[]{:S(2)}, u32[]{:S(2)}) %all-to-all-start.2) | async-done | bytes 487456 | tf_op jit(solution)/shard_map/all_to_all | solution.py:42
  212.0 0.3 fusion.3
  212.4 1.3 collective-permute-start
  213.7 1.4 collective-permute-done
  215.1 1.3 fusion.7
  216.4 0.4 convolution_convert_fusion.2
  216.9 12.1 %all_to_all.32 = bf16[4,17,3584]{2,1,0:T(8,128)(2,1)} all-to-all(bf16[4,17,3584]{2,1,0:T(8,128)(2,1)S(1)} %reshape.93), channel_id=1, replica_groups=mesh['pp'=16,'x'=4,'y'=8] {'x'}, dimensions={0} | all-to-all | bytes 974848 | tf_op jit(solution)/shard_map/all_to_all | solution.py:28
  229.0 1.3 reshape.94
  230.3 0.3 stack.12
  230.6 94.7 %all_to_all.33 = bf16[8,72,3584]{2,1,0:T(8,128)(2,1)S(1)} all-to-all(bf16[8,72,3584]{2,1,0:T(8,128)(2,1)S(1)} %stack.12), channel_id=1, replica_groups=mesh['pp'=16,'x'=4,'y'=8] {'y'}, dimensions={0} | all-to-all | bytes 8257536 | tf_op jit(solution)/shard_map/all_to_all | solution.py:34
  325.3 1.9 copy-done.2
  327.2 1.2 fusion.19
  328.5 8.5 %convolution_convert_fusion = bf16[576,3584]{1,0:T(8,128)(2,1)} fusion(bf16[576,3584]{1,0:T(8,128)(2,1)} %bitcast.60, bf16[1,128,3584]{2,1,0:T(8,128)(2,1)S(1)} %copy-done, bf16[1,3584,128]{2,1,0:T(8,128)(2,1)S(1)} %copy-done.4, f32[576,128]{1,0:T(8,128)S(1)} %fusion.19), kind=kOutput, calls=%fused_computation | convolution fusion | flops 1059471360 | bytes 10387456 | tf_op jit(solution)/shard_map/dot_general | solution.py:39
  337.0 64.0 %reduce-scatter.5.cloned.1.call-done = bf16[72,3584]{1,0:T(8,128)(2,1)} async-done(((bf16[576,3584]{1,0:T(8,128)(2,1)}), bf16[72,3584]{1,0:T(8,128)(2,1)}) %reduce-scatter.5.cloned.1.call-update) | async-done | bytes 516112 | tf_op jit(solution)/shard_map/reduce_scatter | solution.py:40
  400.9 1.2 reshape.96
  402.1 15.2 %all_to_all.34 = bf16[4,17,3584]{2,1,0:T(8,128)(2,1)S(1)} all-to-all(bf16[4,17,3584]{2,1,0:T(8,128)(2,1)S(1)} %reshape.96), channel_id=1, replica_groups=mesh['pp'=16,'x'=4,'y'=8] {'x'}, dimensions={0} | all-to-all | bytes 974848 | tf_op jit(solution)/shard_map/all_to_all | solution.py:42
  417.6 0.3 fusion.4
  417.9 1.0 maximum_bitcast_fusion
  (37 shorter events, 1.5 us)
Async XLA Ops:
  6.5 121.7 %copy-start = (bf16[1,128,3584]{2,1,0:T(8,128)(2,1)S(1)}, bf16[1,128,3584]{2,1,0:T(8,128)(2,1)}, u32[]{:S(2)}) copy-start(bf16[1,128,3584]{2,1,0:T(8,128)(2,1)} %param.13) | copy-start | bytes 2752516
  6.5 187.8 %reduce-scatter.3.cloned.1.call-start = ((), (), s32[]{:S(2)}) async-start(), calls=%async_computation.8 | async-start | bytes 4644864 | tf_op jit(solution)/shard_map/reduce_scatter | solution.py:40
  27.9 99.1 %copy-start.8 = (bf16[1,3584,128]{2,1,0:T(8,128)(2,1)S(1)}, bf16[1,3584,128]{2,1,0:T(8,128)(2,1)}, u32[]{:S(2)}) copy-start(bf16[1,3584,128]{2,1,0:T(8,128)(2,1)} %param.11) | copy-start | bytes 2752516
  125.0 1.9 copy-start.1
  125.0 3.2 copy-start.4
  136.7 63.9 %copy-start.7 = (f32[2,1,64,1]{2,3,1,0:T(1,128)S(1)}, f32[2,1,64,1]{2,3,1,0:T(1,128)}, u32[]{:S(2)}) copy-start(f32[2,1,64,1]{2,3,1,0:T(1,128)} %param.15) | copy-start | bytes 1540
  136.7 75.3 %copy-start.3 = (bf16[1,64,3584]{2,1,0:T(8,128)(2,1)S(1)}, bf16[1,64,3584]{2,1,0:T(8,128)(2,1)}, u32[]{:S(2)}) copy-start(bf16[1,64,3584]{2,1,0:T(8,128)(2,1)} %param.8) | copy-start | bytes 1376260
  196.4 15.4 %all-to-all-start.2 = ((bf16[4,17,3584]{2,1,0:T(8,128)(2,1)}), bf16[4,17,3584]{2,1,0:T(8,128)(2,1)S(1)}, u32[]{:S(2)}, u32[]{:S(2)}) async-start(bf16[4,17,3584]{2,1,0:T(8,128)(2,1)} %reshape.91), calls=%async_computation.3 | async-start | bytes 1376256 | tf_op jit(solution)/shard_map/all_to_all | solution.py:42
  200.6 200.3 %reduce-scatter.5.cloned.1.call-start = ((), (), s32[]{:S(2)}) async-start(), calls=%async_computation.9 | async-start | bytes 4644864 | tf_op jit(solution)/shard_map/reduce_scatter | solution.py:40
  212.3 4.0 copy-start.5
  212.4 2.7 collective-permute-start
  230.6 96.7 %copy-start.9 = (bf16[1,3584,128]{2,1,0:T(8,128)(2,1)S(1)}, bf16[1,3584,128]{2,1,0:T(8,128)(2,1)}, u32[]{:S(2)}) copy-start(bf16[1,3584,128]{2,1,0:T(8,128)(2,1)} %param.11) | copy-start | bytes 2752516
  325.3 1.9 copy-start.2
  337.0 80.9 %copy-start.6 = (bf16[64,3584]{1,0:T(8,128)(2,1)S(1)}, bf16[64,3584]{1,0:T(8,128)(2,1)}, u32[]{:S(2)}) copy-start(bf16[64,3584]{1,0:T(8,128)(2,1)} %copy-done.5) | copy-start | bytes 1376260
Sparse Core Ops, SparseCore 0:
  136.8 57.4 reduce-scatter.2
  337.1 63.7 reduce-scatter.4
